TPU v7x, 256 devices: a whole 4x4x8 slice. The times are simulated.
256 devices in a mesh: row: 32 (over y_lo, z, core), col: 8 (over x, y_hi).
Axes of the slice: x: 4, y: 4 (y_hi: 2, y_lo: 2; y = y_hi * 2 + y_lo), z: 8, core: 2. Of those that a mesh axis runs over, the one named last changes fastest.
Arguments:
- inverse_tiles: bfloat16 [128, 256, 128, 256], P('col', None, 'row'), may hold values from -6 to 6
- factor_panels: bfloat16 [2, 128, 256, 256], P(None, 'row', 'col'), may hold values from -0.0390625 to 0.0390625
- ancestors: int32 [2, 96], replicated, may hold values from 0 to 127, as said below
- valid_flags: int32 [2, 96], replicated, may hold values from 0 to 1, as said below
- block_slot: int32 [128], replicated, may hold values from 0 to 127, each once
Outputs:
- new_panels: float32 [128, 256, 2, 256], P('col', 'row')
Inputs may be any that keep to these rules, and one draw needn't show every extreme that they name: `ancestors`: within one supernode's list all 96 entries name different blocks. `valid_flags`: each list's used entries come first; supernode 0's list is used in full, the others in 64 entries or more.
All inputs are finite; a program needn't handle non-finite values.
Results may differ from a plain program's by a relative error of at most 0.0003.
Values may be sent and summed in bfloat16 or wider, within the bound.
No kernel may reach another device: no remote copies, remote signals or barrier semaphores. Data moves between devices by JAX's collectives and lax.ppermute only.
A program may use at most 64 MiB of HBM per device.

v0:
```python
import jax
import jax.numpy as jnp
from jax import lax
from jax.sharding import PartitionSpec as P


def membership(ancestors, valid_flags, block_slot):
    blocks = jnp.arange(block_slot.shape[0], dtype=jnp.int32)
    pick = (ancestors[:, :, None] == blocks[None, None, :]).astype(jnp.int32)
    slots = jnp.sum(pick * block_slot[None, None, :], axis=2)
    hits = (slots[:, :, None] == blocks[None, None, :]) & (valid_flags[:, :, None] == 1)
    return jnp.any(hits, axis=1)


def panel_product(left, right):
    return jnp.dot(left, right, preferred_element_type=jnp.float32)


def per_device(inverse_tiles, factor_panels, ancestors, valid_flags, block_slot):
    local_rows = inverse_tiles.shape[0]
    width = inverse_tiles.shape[1]
    local_cols = inverse_tiles.shape[2]
    panel_count = factor_panels.shape[0]
    member = membership(ancestors, valid_flags, block_slot)
    col_start = lax.axis_index("row") * local_cols
    row_start = lax.axis_index("col") * local_rows
    col_member = lax.dynamic_slice_in_dim(member, col_start, local_cols, 1)
    row_member = lax.dynamic_slice_in_dim(member, row_start, local_rows, 1)
    left = inverse_tiles.reshape(local_rows * width, local_cols * width)
    masked_local = jnp.where(
        col_member[:, :, None, None], factor_panels, jnp.zeros((), factor_panels.dtype)
    )
    results = []
    for which in range(panel_count):
        whole = lax.all_gather(masked_local[which], "col", axis=1, tiled=True)
        right = whole.reshape(local_cols * width, width)
        partial_value = panel_product(left, right)
        summed = lax.psum_scatter(
            partial_value.reshape(local_rows, width, width), "row", scatter_dimension=1, tiled=True
        )
        results.append(summed)
    stacked = jnp.stack(results, axis=2)
    rowmask = jnp.transpose(row_member)[:, None, :, None]
    return jnp.where(rowmask, -stacked, jnp.zeros((), jnp.float32))


def solution(mesh):
    return jax.shard_map(
        per_device,
        mesh=mesh,
        in_specs=(P("col", None, "row", None), P(None, "row", "col", None), P(), P(), P()),
        out_specs=P("col", "row", None, None),
        check_vma=False,
    )
```

profile of v0, /device:TPU:2, one launch (start us, length us, event | category | flops | bytes accessed | tf_op | source)
XLA Modules:
  0.0 325.4 jit_solution(16764533010754993528)
XLA Ops:
  6.5 0.0 reduce-scatter.3.cloned.1.call-start
  6.5 0.7 broadcast_compare_fusion
  7.2 0.9 select_reduce_fusion
  8.1 0.1 fusion.2
  8.2 0.1 constant_dynamic-slice_fusion
  8.3 1.0 broadcast_select_fusion
  9.3 34.7 %all-gather = bf16[1,4,256,256]{3,2,1,0:T(8,128)(2,1)S(1)} all-gather(bf16[1,4,32,256]{3,2,1,0:T(8,128)(2,1)S(1)} %get-tuple-element.5), channel_id=2, replica_groups=mesh['row'=32,'col'=8] {'col'}, dimensions={2}, use_global_device_ids=true | all-gather | bytes 589824 | tf_op jit(solution)/shard_map/all_gather | solution.py:35
  44.1 9.4 %copy.17 = bf16[512,8,4,256]{3,1,2,0:T(8,128)(2,1)} copy(bf16[512,8,4,256]{3,2,1,0:T(4,128)(2,1)} %bitcast.21) | data formatting | bytes 16777216
  53.4 7.8 %convolution_bitcast_fusion.1 = f32[4096,256]{0,1:T(8,128)} fusion(bf16[1024,256]{1,0:T(8,128)(2,1)S(1)} %bitcast.24, bf16[4096,1024]{1,0:T(8,128)(2,1)} %bitcast.22), kind=kOutput, calls=%fused_computation.1 | convolution fusion | flops 2147483648 | bytes 13107200 | tf_op jit(solution)/shard_map/dot_general | solution.py:16
  61.2 5.6 %copy.15 = f32[4096,256]{1,0:T(8,128)} copy(f32[4096,256]{0,1:T(8,128)} %convolution_bitcast_fusion.1) | data formatting | bytes 8388608 | tf_op jit(solution)/shard_map/reshape | solution.py:39
  66.8 0.0 reduce-scatter.3.cloned.1.call-update
  66.9 0.0 reduce-scatter.5.cloned.1.call-start
  66.9 35.3 %all-gather.1 = bf16[1,4,256,256]{3,2,1,0:T(8,128)(2,1)S(1)} all-gather(bf16[1,4,32,256]{3,2,1,0:T(8,128)(2,1)S(1)} %get-tuple-element.6), channel_id=3, replica_groups=mesh['row'=32,'col'=8] {'col'}, dimensions={2}, use_global_device_ids=true | all-gather | bytes 589824 | tf_op jit(solution)/shard_map/all_gather | solution.py:35
  102.2 7.8 %convolution_bitcast_fusion = f32[4096,256]{0,1:T(8,128)} fusion(bf16[1024,256]{1,0:T(8,128)(2,1)S(1)} %bitcast.25, bf16[4096,1024]{1,0:T(8,128)(2,1)} %bitcast.23), kind=kOutput, calls=%fused_computation | convolution fusion | flops 2147483648 | bytes 13107200 | tf_op jit(solution)/shard_map/dot_general | solution.py:16
  110.0 5.6 %copy.16 = f32[4096,256]{1,0:T(8,128)} copy(f32[4096,256]{0,1:T(8,128)} %convolution_bitcast_fusion) | data formatting | bytes 8388608 | tf_op jit(solution)/shard_map/reshape | solution.py:39
  115.6 0.0 reduce-scatter.5.cloned.1.call-update
  115.7 0.1 dynamic-slice_bitcast_fusion
  115.7 78.5 %reduce-scatter.3.cloned.1.call-done = f32[16,8,256]{2,1,0:T(8,128)} async-done(((f32[16,256,256]{2,1,0:T(8,128)}), f32[16,8,256]{2,1,0:T(8,128)}) %reduce-scatter.3.cloned.1.call-update) | async-done | bytes 131088 | tf_op jit(solution)/shard_map/reduce_scatter | solution.py:38
  194.3 122.3 %reduce-scatter.5.cloned.1.call-done = f32[16,8,256]{2,1,0:T(8,128)} async-done(((f32[16,256,256]{2,1,0:T(8,128)}), f32[16,8,256]{2,1,0:T(8,128)}) %reduce-scatter.5.cloned.1.call-update) | async-done | bytes 131088 | tf_op jit(solution)/shard_map/reduce_scatter | solution.py:38
  316.6 1.1 fusion
  317.6 0.9 copy.14
  (1 shorter events, 0.0 us)
Async XLA Ops:
  6.5 187.7 %reduce-scatter.3.cloned.1.call-start = ((), (), s32[]{:S(2)}) async-start(), calls=%async_computation.2 | async-start | bytes 4325376 | tf_op jit(solution)/shard_map/reduce_scatter | solution.py:38
  66.9 249.7 %reduce-scatter.5.cloned.1.call-start = ((), (), s32[]{:S(2)}) async-start(), calls=%async_computation.3 | async-start | bytes 4325376 | tf_op jit(solution)/shard_map/reduce_scatter | solution.py:38
Sparse Core Ops, SparseCore 0:
  67.0 127.2 reduce-scatter.2
  196.8 119.7 reduce-scatter.4
where the time goes:
time: 326 us; the launch traced here: 325 us
  waiting for transfers between devices  201 us (62%)
  blocking collectives  70.1 us (22%)
  local copies, waits for them, and re-layouts  21.6 us (7%)
  matrix products  15.6 us (5%)
  between operations  13.4 us (4%)
  other arithmetic  3.75 us (1%)
    reduce_scatter x2, waiting for transfers between devices, per_device(): lax.psum_scatter(partial_value.reshape(local_rows, width, width), 'row',...  201 us
    all_gather x2, blocking collectives, per_device(): whole = lax.all_gather(masked_local[which], 'col', axis=1, tiled=True)  70.1 us
    dot_general x2, matrix products, panel_product(): return jnp.dot(left, right, preferred_element_type=jnp.float32)  15.6 us
    reshape x2, local copies, waits for them, and re-layouts, per_device(): partial_value.reshape(local_rows, width, width)  11.2 us
    unnamed x1, local copies, waits for them, and re-layouts  9.35 us
  transfers between devices with their start and end apart: 2, of which 2 were waited for; matrix products, arithmetic and copies ran while one was open for 4% of the time, Pallas kernels for 0%

commit v1 on v0

--- a/solution.py
+++ b/solution.py
@@ -32,7 +32,11 @@
     )
     results = []
     for which in range(panel_count):
-        whole = lax.all_gather(masked_local[which], "col", axis=1, tiled=True)
+        block = masked_local[which]
+        devices = lax.axis_size("col")
+        pieces = jnp.stack([block for _ in range(devices)])
+        pieces = lax.all_to_all(pieces, "col", split_axis=0, concat_axis=0)
+        whole = jnp.concatenate(pieces, axis=1)
         right = whole.reshape(local_cols * width, width)
         partial_value = panel_product(left, right)
         summed = lax.psum_scatter(

time: 326 us -> 299 us (0.917)
  blocking collectives: 70.1 us -> 15.7 us
  waiting for transfers between devices: 201 us -> 220 us
  starting transfers between devices: 0.04 us -> 7.51 us
    all_gather x2 -> x0, blocking collectives: 70.1 us -> none  [per_device(): whole = lax.all_gather(masked_local[which], 'col', axis=1, tiled=True)]
    reduce_scatter x2, waiting for transfers between devices: 201 us -> 219 us  [per_device(): lax.psum_scatter(partial_value.reshape(local_rows, width, width), 'row',...]
    all_to_all x0 -> x1, blocking collectives: none -> 15.7 us  [per_device(): pieces = lax.all_to_all(pieces, 'col', split_axis=0, concat_axis=0)]
    all_to_all x0 -> x1, starting transfers between devices: none -> 7.46 us  [per_device(): pieces = lax.all_to_all(pieces, 'col', split_axis=0, concat_axis=0)]
  transfers between devices with their start and end apart: 2 -> 3, of which waited for: 2 -> 3; matrix products, arithmetic and copies ran while one was open for 4% -> 8% of each run, Pallas kernels for 0% -> 0%
where the time goes in v1:
time: 299 us; the launch traced here: 298 us
  waiting for transfers between devices  220 us (74%)
  local copies, waits for them, and re-layouts  22.7 us (8%)
  blocking collectives  15.7 us (5%)
  matrix products  15.5 us (5%)
  between operations  13.5 us (5%)
  starting transfers between devices  7.51 us (3%)
  other arithmetic  3.75 us (1%)
    reduce_scatter x2, waiting for transfers between devices, per_device(): lax.psum_scatter(partial_value.reshape(local_rows, width, width), 'row',...  219 us
    all_to_all x1, blocking collectives, per_device(): pieces = lax.all_to_all(pieces, 'col', split_axis=0, concat_axis=0)  15.7 us
    dot_general x2, matrix products, panel_product(): return jnp.dot(left, right, preferred_element_type=jnp.float32)  15.5 us
    reshape x2, local copies, waits for them, and re-layouts, per_device(): partial_value.reshape(local_rows, width, width)  11.2 us
    unnamed x1, local copies, waits for them, and re-layouts  9.35 us
    all_to_all x1, starting transfers between devices, per_device(): pieces = lax.all_to_all(pieces, 'col', split_axis=0, concat_axis=0)  7.46 us
  transfers between devices with their start and end apart: 3, of which 3 were waited for; matrix products, arithmetic and copies ran while one was open for 8% of the time, Pallas kernels for 0%

profile of v1, /device:TPU:2, one launch (start us, length us, event | category | flops | bytes accessed | tf_op | source)
XLA Modules:
  0.0 298.1 jit_solution(7570672549993864059)
XLA Ops:
  6.5 0.7 broadcast_compare_fusion
  7.2 0.9 select_reduce_fusion
  8.1 0.1 fusion.2
  8.2 0.1 constant_dynamic-slice_fusion
  8.3 1.0 broadcast_select_fusion
  9.3 0.9 stack.17
  10.2 7.5 %all-to-all-start.1 = ((bf16[8,4,32,256]{3,2,1,0:T(8,128)(2,1)}), bf16[8,4,32,256]{3,2,1,0:T(8,128)(2,1)S(1)}, u32[]{:S(2)}, u32[]{:S(2)}) async-start(bf16[8,4,32,256]{3,2,1,0:T(8,128)(2,1)} %stack.17), calls=%async_computation.2 | async-start | bytes 1048576 | tf_op jit(solution)/shard_map/all_to_all | solution.py:38
  17.7 0.0 reduce-scatter.5.cloned.1.call-start
  17.7 9.4 %copy.24 = bf16[512,8,4,256]{3,1,2,0:T(8,128)(2,1)} copy(bf16[512,8,4,256]{3,2,1,0:T(4,128)(2,1)} %bitcast.29) | data formatting | bytes 16777216
  27.0 0.3 all-to-all-done.1
  27.3 7.7 %convolution_bitcast_fusion = f32[4096,256]{0,1:T(8,128)} fusion(bf16[1024,256]{1,0:T(8,128)(2,1)S(1)} %bitcast.33, bf16[4096,1024]{1,0:T(8,128)(2,1)} %bitcast.30), kind=kOutput, calls=%fused_computation | convolution fusion | flops 2147483648 | bytes 13107200 | tf_op jit(solution)/shard_map/dot_general | solution.py:16
  35.1 5.6 %copy.23 = f32[4096,256]{1,0:T(8,128)} copy(f32[4096,256]{0,1:T(8,128)} %convolution_bitcast_fusion) | data formatting | bytes 8388608 | tf_op jit(solution)/shard_map/reshape | solution.py:43
  40.7 0.0 reduce-scatter.5.cloned.1.call-update
  40.7 0.0 reduce-scatter.3.cloned.1.call-start
  40.7 0.1 stack.15
  40.8 15.7 %all_to_all.10 = bf16[8,4,32,256]{3,2,1,0:T(8,128)(2,1)S(1)} all-to-all(bf16[8,4,32,256]{3,2,1,0:T(8,128)(2,1)S(1)} %stack.15), channel_id=1, replica_groups=mesh['row'=32,'col'=8] {'col'}, dimensions={0} | all-to-all | bytes 1048576 | tf_op jit(solution)/shard_map/all_to_all | solution.py:38
  56.5 7.7 %convolution_bitcast_fusion.1 = f32[4096,256]{0,1:T(8,128)} fusion(bf16[1024,256]{1,0:T(8,128)(2,1)S(1)} %bitcast.32, bf16[4096,1024]{1,0:T(8,128)(2,1)} %bitcast.31), kind=kOutput, calls=%fused_computation.1 | convolution fusion | flops 2147483648 | bytes 13107200 | tf_op jit(solution)/shard_map/dot_general | solution.py:16
  64.2 5.6 %copy.22 = f32[4096,256]{1,0:T(8,128)} copy(f32[4096,256]{0,1:T(8,128)} %convolution_bitcast_fusion.1) | data formatting | bytes 8388608 | tf_op jit(solution)/shard_map/reshape | solution.py:43
  69.8 0.0 reduce-scatter.3.cloned.1.call-update
  69.9 0.1 dynamic-slice_bitcast_fusion
  70.0 97.0 %reduce-scatter.5.cloned.1.call-done = f32[16,8,256]{2,1,0:T(8,128)} async-done(((f32[16,256,256]{2,1,0:T(8,128)}), f32[16,8,256]{2,1,0:T(8,128)}) %reduce-scatter.5.cloned.1.call-update) | async-done | bytes 131088 | tf_op jit(solution)/shard_map/reduce_scatter | solution.py:42
  166.9 122.3 %reduce-scatter.3.cloned.1.call-done = f32[16,8,256]{2,1,0:T(8,128)} async-done(((f32[16,256,256]{2,1,0:T(8,128)}), f32[16,8,256]{2,1,0:T(8,128)}) %reduce-scatter.3.cloned.1.call-update) | async-done | bytes 131088 | tf_op jit(solution)/shard_map/reduce_scatter | solution.py:42
  289.2 1.1 fusion
  290.3 0.9 copy.21
  (3 shorter events, 0.1 us)
Async XLA Ops:
  10.2 17.1 %all-to-all-start.1 = ((bf16[8,4,32,256]{3,2,1,0:T(8,128)(2,1)}), bf16[8,4,32,256]{3,2,1,0:T(8,128)(2,1)S(1)}, u32[]{:S(2)}, u32[]{:S(2)}) async-start(bf16[8,4,32,256]{3,2,1,0:T(8,128)(2,1)} %stack.17), calls=%async_computation.2 | async-start | bytes 1048576 | tf_op jit(solution)/shard_map/all_to_all | solution.py:38
  17.7 149.2 %reduce-scatter.5.cloned.1.call-start = ((), (), s32[]{:S(2)}) async-start(), calls=%async_computation.5 | async-start | bytes 4325376 | tf_op jit(solution)/shard_map/reduce_scatter | solution.py:42
  40.7 248.5 %reduce-scatter.3.cloned.1.call-start = ((), (), s32[]{:S(2)}) async-start(), calls=%async_computation.4 | async-start | bytes 4325376 | tf_op jit(solution)/shard_map/reduce_scatter | solution.py:42
Sparse Core Ops, SparseCore 0:
  40.8 126.0 reduce-scatter.4
  169.4 119.7 reduce-scatter.2
